TPU v7x, 32 devices: a whole 2x2x4 slice. The times are simulated.
32 devices in a mesh: gx: 4 (over x, core), gy: 8 (over z, y).
Axes of the slice: x: 2, y: 2, z: 4, core: 2. Of those that a mesh axis runs over, the one named last changes fastest.
Arguments:
- queries: bfloat16 [256, 2560], P('gx'), may hold values from -8 to 8
- token_key_value: bfloat16 [256, 1024], P('gx'), may hold values from -6 to 6
- group_cached_keys: bfloat16 [4, 32768, 512], P('gx', 'gy'), may hold values from -8 to 8
- group_cached_values: bfloat16 [4, 32768, 512], P('gx', 'gy'), may hold values from -6 to 6
- owners: int32 [4, 32768], P('gx', 'gy'), may hold values from 0 to 63, never falling along the last dimension, each value on 1 to 16384 neighbouring positions
- out_weight: bfloat16 [2560, 2560], P(None, 'gy'), may hold values from -0.125 to 0.125
- residual: bfloat16 [256, 2560], P('gx', 'gy'), may hold values from -6 to 6
- norm_gain: bfloat16 [2560], P('gy'), may hold values from 0.099609375 to 1.8984375
- expert_ids: int32 [256, 6], replicated, may hold values from 0 to 63, all different within a row; in each aligned block of 64 rows (0 to 63, 64 to 127, ...) at most 12 rows name the same one
- gate_logits: float32 [256, 6], replicated, may hold values from -0.5 to 0.5
- w_gate_up: bfloat16 [64, 2560, 3072], P('gx', 'gy'), may hold values from -0.125 to 0.125
- w_down: bfloat16 [64, 1536, 2560], P('gx', None, 'gy'), may hold values from -0.15625 to 0.15625
Outputs:
- layer_out: float32 [256, 2560], P('gx', 'gy')
Inputs may be any that keep to these rules, and one draw needn't show every extreme that they name: `owners`: each request's positions form one run; every request owns at least one position and at most 16384, and some request owns exactly 16384. `expert_ids`: within each group of 64 requests no expert is named by more than 12 requests, a bound that some block reaches.
All inputs are finite; a program needn't handle non-finite values.
Results may differ from a plain program's by a relative error of at most 0.0075.
Values may be sent and summed in bfloat16 or wider, within the bound.
No kernel may reach another device: no remote copies, remote signals or barrier semaphores. Data moves between devices by JAX's collectives and lax.ppermute only.
A program may use at most 192 MiB of HBM per device.

v0:
```python
import jax
import jax.numpy as jnp
from jax import lax
from jax.sharding import PartitionSpec as P

D = 2560
QUERY_HEADS = 20
KEY_VALUE_HEADS = 4
HEAD_SIZE = 128
E = 64
TOPK = 6
CAPS = 12
minimal_score = -1e30
norm_epsilon = 1e-05


def merged(part, axis, combine):
    gathered = jax.tree.map(lambda a: lax.all_gather(a, axis), part)

    def take(source):
        return jax.tree.map(lambda a: lax.dynamic_index_in_dim(a, source, 0, False), gathered)

    return lax.fori_loop(
        1, lax.axis_size(axis), lambda source, state: combine(state, take(source)), take(0)
    )


def merge_partial(earlier_part, later_part):
    max_one, den_one, acc_one = earlier_part
    max_two, den_two, acc_two = later_part
    peak = jnp.maximum(max_one, max_two)
    scale_one = jnp.exp(max_one - peak)
    scale_two = jnp.exp(max_two - peak)
    return (
        peak,
        den_one * scale_one + den_two * scale_two,
        acc_one * scale_one[..., None] + acc_two * scale_two[..., None],
    )


def slot_ranks(flat_ids, num_experts):
    onehot = (flat_ids[..., None] == lax.iota(jnp.int32, num_experts)).astype(jnp.int32)
    earlier = jnp.cumsum(onehot, axis=-2) - onehot
    return jnp.sum(earlier * onehot, axis=-1)


def attend_local(queries, group_cached_keys, group_cached_values, owners):
    request_rows = queries.shape[0]
    query_heads_per_group = QUERY_HEADS // KEY_VALUE_HEADS
    positions = group_cached_keys.shape[0]
    block_length = min(positions, 512)
    block_count = positions // block_length
    key_block_list = group_cached_keys.reshape(
        block_count, block_length, KEY_VALUE_HEADS, HEAD_SIZE
    )
    value_block_list = group_cached_values.reshape(
        block_count, block_length, KEY_VALUE_HEADS, HEAD_SIZE
    )
    owner_blocks = owners.reshape(block_count, block_length)
    scaling = HEAD_SIZE ** (-0.5)
    request_ids = lax.iota(jnp.int32, request_rows)

    def visit_block(state_in, inputs):
        run_max, run_den, run_acc = state_in
        key_block, value_block, owning_block = inputs
        picked_experts = queries[owning_block].reshape(
            block_length, KEY_VALUE_HEADS, query_heads_per_group, HEAD_SIZE
        )
        scores = (
            jnp.einsum(
                "tkgd,tkd->tkg", picked_experts, key_block, preferred_element_type=jnp.float32
            )
            * scaling
        )
        member = owning_block[:, None] == request_ids[None, :]
        block_max = jnp.max(
            jnp.where(member[:, :, None, None], scores[:, None], minimal_score), axis=0
        )
        new_max = jnp.maximum(run_max, block_max)
        prob_block = jnp.exp(scores - new_max[owning_block]).astype(jnp.bfloat16)
        spread = jnp.where(
            member[:, :, None, None], prob_block[:, None], jnp.zeros((), jnp.bfloat16)
        )
        rescale = jnp.exp(run_max - new_max)
        run_den = run_den * rescale + jnp.sum(spread.astype(jnp.float32), axis=0)
        run_acc = run_acc * rescale[..., None] + jnp.einsum(
            "trkg,tkd->rkgd", spread, value_block, preferred_element_type=jnp.float32
        )
        return ((new_max, run_den, run_acc), None)

    initial = (
        jnp.full(
            (request_rows, KEY_VALUE_HEADS, query_heads_per_group), minimal_score, jnp.float32
        ),
        jnp.zeros((request_rows, KEY_VALUE_HEADS, query_heads_per_group), jnp.float32),
        jnp.zeros((request_rows, KEY_VALUE_HEADS, query_heads_per_group, HEAD_SIZE), jnp.float32),
    )
    return lax.scan(visit_block, initial, (key_block_list, value_block_list, owner_blocks))[0]


def expert_block(tokens, w_gate_up, w_down):
    hidden_units = w_down.shape[1]
    gate_up = jnp.einsum("sekd,edf->sekf", tokens, w_gate_up, preferred_element_type=jnp.float32)
    gate_up = lax.psum(gate_up, "gy")
    active = (jax.nn.silu(gate_up[..., :hidden_units]) * gate_up[..., hidden_units:]).astype(
        jnp.bfloat16
    )
    return jnp.einsum("sekf,efd->sekd", active, w_down, preferred_element_type=jnp.float32).astype(
        jnp.bfloat16
    )


def shards(
    queries,
    token_key_value,
    group_cached_keys,
    group_cached_values,
    owners,
    out_weight,
    residual,
    norm_gain,
    expert_ids,
    gate_logits,
    w_gate_up,
    w_down,
):
    request_rows = queries.shape[0]
    query_heads_per_group = QUERY_HEADS // KEY_VALUE_HEADS
    key_value_width = token_key_value.shape[1] // 2
    scaling = HEAD_SIZE ** (-0.5)
    run_max, run_den, run_acc = attend_local(
        queries, group_cached_keys[0], group_cached_values[0], owners[0]
    )
    query_head_rows = queries.reshape(
        request_rows, KEY_VALUE_HEADS, query_heads_per_group, HEAD_SIZE
    )
    appended_keys = token_key_value[:, :key_value_width].reshape(
        request_rows, KEY_VALUE_HEADS, HEAD_SIZE
    )
    appended_values = token_key_value[:, key_value_width:]
    own_score = (
        jnp.einsum(
            "rkgd,rkd->rkg", query_head_rows, appended_keys, preferred_element_type=jnp.float32
        )
        * scaling
    )
    run_max, run_den, run_acc = merged((run_max, run_den, run_acc), "gy", merge_partial)
    peak = jnp.maximum(run_max, own_score)
    rescale = jnp.exp(run_max - peak)
    own_prob = lax.optimization_barrier(jnp.exp(own_score - peak).astype(jnp.bfloat16)).astype(
        jnp.float32
    )
    denominator = run_den * rescale + own_prob
    incoming_values = appended_values.astype(jnp.float32).reshape(
        request_rows, KEY_VALUE_HEADS, 1, HEAD_SIZE
    )
    numerator = run_acc * rescale[..., None] + own_prob[..., None] * incoming_values
    attention = (
        (numerator / denominator[..., None])
        .astype(jnp.bfloat16)
        .reshape(request_rows, QUERY_HEADS * HEAD_SIZE)
    )
    projected = jnp.dot(attention, out_weight, preferred_element_type=jnp.float32)
    hidden = (residual.astype(jnp.float32) + projected).astype(jnp.bfloat16)
    hidden_f = hidden.astype(jnp.float32)
    squares = lax.psum(jnp.sum(hidden_f * hidden_f, axis=1), "gy")
    inv_rms = lax.rsqrt(squares / D + norm_epsilon)
    normed = (hidden_f * inv_rms[:, None] * norm_gain.astype(jnp.float32)[None, :]).astype(
        jnp.bfloat16
    )
    mixing = jax.nn.softmax(gate_logits, axis=-1)
    num_gx = lax.axis_size("gx")
    group_index = lax.axis_index("gx")
    per_row = w_gate_up.shape[0]
    columns_here = normed.shape[1]
    my_ids = lax.dynamic_slice_in_dim(
        expert_ids, group_index * request_rows, request_rows, 0
    ).reshape(-1)
    my_mix = lax.dynamic_slice_in_dim(mixing, group_index * request_rows, request_rows, 0)
    places = my_ids * CAPS + slot_ranks(my_ids, E)
    outgoing = (
        jnp.zeros((E * CAPS, columns_here), jnp.bfloat16)
        .at[places]
        .set(jnp.repeat(normed, TOPK, axis=0))
    )
    returned = lax.all_to_all(
        expert_block(
            lax.all_to_all(
                outgoing.reshape(num_gx, per_row, CAPS, columns_here),
                "gx",
                split_axis=0,
                concat_axis=0,
                tiled=True,
            ),
            w_gate_up,
            w_down,
        ),
        "gx",
        split_axis=0,
        concat_axis=0,
        tiled=True,
    )
    picked = (
        returned.reshape(E * CAPS, columns_here)[places]
        .astype(jnp.float32)
        .reshape(request_rows, TOPK, columns_here)
    )
    routed = jnp.sum(my_mix[..., None] * picked, axis=1)
    return hidden_f + routed


def solution(mesh):
    placed = (
        P("gx", None),
        P("gx", None),
        P("gx", "gy", None),
        P("gx", "gy", None),
        P("gx", "gy"),
        P(None, "gy"),
        P("gx", "gy"),
        P("gy"),
        P(),
        P(),
        P("gx", "gy", None),
        P("gx", None, "gy"),
    )
    return jax.shard_map(
        shards, mesh=mesh, in_specs=placed, out_specs=P("gx", "gy"), check_vma=False
    )
```

profile of v0, /device:TPU:0, one launch (start us, length us, event | category | flops | bytes accessed | tf_op | source)
XLA Modules:
  0.0 817.4 jit_solution(4890092526414652480)
XLA Ops:
  6.5 7.0 reshape.208
  13.6 7.0 reshape_squeeze.10
  22.4 178.0 %while.35 = (s32[]{:T(128)}, f32[64,4,5]{2,1,0:T(4,128)S(1)}, f32[64,4,5]{2,1,0:T(4,128)S(1)}, f32[64,4,5,128]{3,0,2,1:T(8,128)}, s32[8,512]{1,0:T(8,128)}, /*in...) while((s32[]{:T(128)}, f32[64,4,5]{2,1,0:T(4,128)S(1)}, ...), condition=%wide.region_3.4_spmd.clone, body=%wide.region_0.3_spmd.clone.sunk | while | flops 176462592 | bytes 21555320 | solution.py:98
  23.1 3.6 gather_fusion
  26.7 4.5 copy.169
  44.4 3.6 gather_fusion
  48.0 4.5 copy.169
  66.8 3.6 gather_fusion
  70.4 4.5 copy.169
  92.8 4.5 copy.169
  115.2 4.5 copy.169
  137.6 4.5 copy.169
  160.0 4.5 copy.169
  182.4 4.5 copy.169
  202.2 38.6 %all-gather = f32[512,4,5]{2,1,0:T(4,128)S(1)} all-gather(f32[64,4,5]{2,1,0:T(4,128)S(1)} %get-tuple-element.232), channel_id=2, replica_groups=mesh['gx'=4,'gy'=8] {'gy'}, dimensions={0}, use_global_device_ids=true | all-gather | bytes 46080 | tf_op jit(solution)/shard_map/all_gather | solution.py:18
  240.9 35.2 %all-gather.1 = f32[512,4,5]{2,1,0:T(4,128)S(1)} all-gather(f32[64,4,5]{2,1,0:T(4,128)S(1)} %get-tuple-element.233), channel_id=3, replica_groups=mesh['gx'=4,'gy'=8] {'gy'}, dimensions={0}, use_global_device_ids=true | all-gather | bytes 46080 | tf_op jit(solution)/shard_map/all_gather | solution.py:18
  282.6 27.2 %all-gather.5.cloned.1.call-done = f32[512,4,5,128]{3,0,2,1:T(8,128)} async-done(((f32[64,4,5,128]{3,0,2,1:T(8,128)}), f32[512,4,5,128]{3,0,2,1:T(8,128)}) %all-gather.5.cloned.1.call-update) | async-done | bytes 5242896 | tf_op jit(solution)/shard_map/all_gather | solution.py:18
  311.4 20.6 %while.34 = (s32[]{:T(128)}, f32[64,4,5]{0,1,2:T(4,128)S(1)}, f32[64,4,5]{0,1,2:T(4,128)S(1)}, f32[64,4,5,128]{3,2,1,0:T(8,128)S(1)}, f32[8,64,4,5]{1,2,3,0:T(4,...) while((s32[]{:T(128)}, f32[64,4,5]{0,1,2:T(4,128)S(1)}, ...), condition=%wide.region_5.6_spmd, body=%wide.region_4.5_spmd.sunk | while | flops 499205 | bytes 3348631 | solution.py:23
  336.7 19.3 %psum.14 = f32[64]{0:T(128)S(1)} all-reduce(f32[64]{0:T(128)S(1)} %get-tuple-element.365), channel_id=1, replica_groups=mesh['gx'=4,'gy'=8] {'gy'}, use_global_device_ids=true, to_apply=%region_12.13 | all-reduce | flops 64 | bytes 512 | tf_op jit(solution)/shard_map/psum | solution.py:166
  358.7 12.1 %all_to_all.10 = bf16[4,16,12,320]{3,1,2,0:T(8,128)(2,1)S(1)} all-to-all(bf16[4,16,12,320]{3,1,2,0:T(8,128)(2,1)S(1)} %copy.108), channel_id=1, replica_groups=mesh['gx'=4,'gy'=8] {'gx'}, dimensions={0} | all-to-all | bytes 983040 | tf_op jit(solution)/shard_map/all_to_all | solution.py:188
  370.8 16.6 %fusion.23 = f32[4,16,12,3072]{3,2,0,1:T(8,128)} fusion(bf16[16,320,3072]{2,1,0:T(8,128)(2,1)} %param.26, bf16[4,16,12,320]{3,1,2,0:T(8,128)(2,1)S(1)} %all_to_all.10), kind=kOutput, calls=%fused_computation.44 | convolution fusion | flops 1509949440 | bytes 41385984 | tf_op jit(solution)/shard_map/sekd,edf->sekf/dot_general | solution.py:103
  388.2 393.0 %all-reduce.2.cloned.1.call-done = f32[4,16,12,3072]{3,2,0,1:T(8,128)} async-done(((f32[4,16,12,3072]{3,2,0,1:T(8,128)}), f32[4,16,12,3072]{3,2,0,1:T(8,128)}) %all-reduce.2.cloned.1.call-update) | async-done | bytes 9437200 | tf_op jit(solution)/shard_map/psum | solution.py:104
  781.2 11.6 %fusion.34 = bf16[4,16,12,320]{3,2,0,1:T(8,128)(2,1)S(1)} fusion(bf16[16,1536,320]{1,2,0:T(8,128)(2,1)} %param.27, f32[4,16,12,3072]{3,2,0,1:T(8,128)} %all-reduce.2.cloned.1.call-done), kind=kOutput, calls=%fused_computation.49 | convolution fusion | flops 762298368 | bytes 25657344 | tf_op jit(solution)/shard_map/sekf,efd->sekd/dot_general | solution.py:108
  797.7 9.2 %all-to-all-done.1 = bf16[4,16,12,320]{3,1,2,0:T(8,128)(2,1)S(1)} async-done(((bf16[4,16,12,320]{3,1,2,0:T(8,128)(2,1)}), bf16[4,16,12,320]{3,1,2,0:T(8,128)(2,1)S(1)}, u32[]{:S(2)}, u32[]{:S(2)}) %all-to-all-start.1) | async-done | bytes 491552 | tf_op jit(solution)/shard_map/all_to_all | solution.py:186
  (300 shorter events, 178.9 us)
Async XLA Ops:
  6.5 329.4 %copy-start = (bf16[2560,320]{0,1:T(8,128)(2,1)S(1)}, bf16[2560,320]{0,1:T(8,128)(2,1)}, u32[]{:S(2)}) copy-start(bf16[2560,320]{0,1:T(8,128)(2,1)} %param.21) | copy-start | bytes 4915204
  6.5 303.3 %all-gather.5.cloned.1.call-start = ((), (), s32[]{:S(2)}) async-start(), calls=%async_computation.3 | async-start | bytes 5898240 | tf_op jit(solution)/shard_map/all_gather | solution.py:18
  13.6 7.5 copy-start.6
  13.6 8.8 %copy-start.1 = (bf16[64,2560]{1,0:T(8,128)(2,1)S(1)}, bf16[64,2560]{1,0:T(8,128)(2,1)}, u32[]{:S(2)}) copy-start(bf16[64,2560]{1,0:T(8,128)(2,1)} %param.16) | copy-start | bytes 983044
  22.4 179.4 %copy-start.7 = (s32[256,6]{0,1:T(8,128)S(1)}, s32[256,6]{0,1:T(8,128)}, u32[]{:S(2)}) copy-start(s32[256,6]{0,1:T(8,128)} %param.24) | copy-start | bytes 18436
  200.4 78.9 %copy-start.3 = (bf16[64,1024]{1,0:T(8,128)(2,1)S(1)}, bf16[64,1024]{1,0:T(8,128)(2,1)}, u32[]{:S(2)}) copy-start(bf16[64,1024]{1,0:T(8,128)(2,1)} %param.17) | copy-start | bytes 393220
  200.5 80.5 %copy-start.8 = (bf16[320]{0:T(512)(128)(2,1)S(1)}, bf16[320]{0:T(512)(128)(2,1)}, u32[]{:S(2)}) copy-start(bf16[320]{0:T(512)(128)(2,1)} %param.23) | copy-start | bytes 1924
  200.5 580.7 %all-reduce.2.cloned.1.call-start = ((), (), s32[]{:S(2)}) async-start(), calls=%async_computation.2 | async-start | bytes 25165824 | tf_op jit(solution)/shard_map/psum | solution.py:104
  276.2 1.0 copy-start.2
  311.4 24.6 %copy-start.4 = (bf16[64,320]{1,0:T(8,128)(2,1)S(1)}, bf16[64,320]{1,0:T(8,128)(2,1)}, u32[]{:S(2)}) copy-start(bf16[64,320]{1,0:T(8,128)(2,1)} %param.22) | copy-start | bytes 122884
  387.4 0.7 copy-start.5
  793.9 13.0 %all-to-all-start.1 = ((bf16[4,16,12,320]{3,1,2,0:T(8,128)(2,1)}), bf16[4,16,12,320]{3,1,2,0:T(8,128)(2,1)S(1)}, u32[]{:S(2)}, u32[]{:S(2)}) async-start(bf16[4,16,12,320]{3,1,2,0:T(8,128)(2,1)} %copy.110), calls=%async_computation.1 | async-start | bytes 1179648 | tf_op jit(solution)/shard_map/all_to_all | solution.py:186
Sparse Core Ops, SparseCore 0:
  200.6 109.1 all-gather.4
  387.6 393.5 all-reduce.1
where the time goes:
time: 821 us; the launch traced here: 817 us
  waiting for transfers between devices  429 us (52%)
  local copies, waits for them, and re-layouts  151 us (18%)
  blocking collectives  105 us (13%)
  other arithmetic  64.6 us (8%)
  matrix products  48.9 us (6%)
  between operations  13.7 us (2%)
    psum x1, waiting for transfers between devices, expert_block(): gate_up = lax.psum(gate_up, 'gy')  393 us
    all_gather x2, blocking collectives, merged(): gathered = jax.tree.map(lambda a: lax.all_gather(a, axis), part)  73.9 us
    while x24, local copies, waits for them, and re-layouts  48.4 us
    while x16, other arithmetic  35.7 us
    gather x8, local copies, waits for them, and re-layouts, visit_block(): queries[owning_block]  28.5 us
    all_gather x1, waiting for transfers between devices, merged(): gathered = jax.tree.map(lambda a: lax.all_gather(a, axis), part)  27.2 us
    gather x16, local copies, waits for them, and re-layouts, visit_block(): prob_block = jnp.exp(scores - new_max[owning_block]).astype(jnp.bfloat16)  19.4 us
    psum x1, blocking collectives, shards(): squares = lax.psum(jnp.sum(hidden_f * hidden_f, axis=1), 'gy')  19.3 us
  transfers between devices with their start and end apart: 3, of which 3 were waited for; matrix products, arithmetic and copies ran while one was open for 1% of the time, Pallas kernels for 0%

commit v1 on v0

--- a/solution.py
+++ b/solution.py
@@ -12,6 +12,29 @@
 CAPS = 12
 minimal_score = -1e30
 norm_epsilon = 1e-05
+
+
+def edge_raise(view, chip_axis):
+    newest = lax.axis_size(chip_axis)
+    value_now, big = (newest, lax.axis_index(chip_axis))
+    now = list(view.shape)
+    mat_out = view.shape[0] // value_now
+    now[0] = mat_out
+    current_value = now[0]
+    now[0] = current_value * value_now
+    taken_in = jnp.zeros(now, view.dtype)
+    pp = 0
+    while pp < value_now:
+        everything = lax.dynamic_slice_in_dim(view, (big ^ pp) * mat_out, mat_out, axis=0)
+        if pp:
+            everything = lax.ppermute(
+                everything, chip_axis, perm=[(u, u ^ pp) for u in range(value_now)]
+            )
+        taken_in = lax.dynamic_update_slice_in_dim(
+            taken_in, everything, (big ^ pp) * current_value, axis=0
+        )
+        pp = pp + 1
+    return taken_in
 
 
 def merged(part, axis, combine):
@@ -183,7 +206,7 @@
         .at[places]
         .set(jnp.repeat(normed, TOPK, axis=0))
     )
-    returned = lax.all_to_all(
+    returned = edge_raise(
         expert_block(
             lax.all_to_all(
                 outgoing.reshape(num_gx, per_row, CAPS, columns_here),
@@ -195,10 +218,7 @@
             w_gate_up,
             w_down,
         ),
-        "gx",
-        split_axis=0,
-        concat_axis=0,
-        tiled=True,
+        chip_axis="gx",
     )
     picked = (
         returned.reshape(E * CAPS, columns_here)[places]

time: 821 us -> 819 us (level)
    all_to_all x1 -> x0, waiting for transfers between devices: 9.22 us -> none  [shards(): lax.all_to_all(expert_block(lax.all_to_all(outgoing.reshape(num_gx, per_r...]
  transfers between devices with their start and end apart: 3 -> 5, of which waited for: 3 -> 4; matrix products, arithmetic and copies ran while one was open for 1% -> 1% of each run, Pallas kernels for 0% -> 0%
where the time goes in v1:
time: 819 us; the launch traced here: 815 us
  waiting for transfers between devices  428 us (52%)
  local copies, waits for them, and re-layouts  152 us (19%)
  blocking collectives  105 us (13%)
  other arithmetic  64.6 us (8%)
  matrix products  48.9 us (6%)
  between operations  13.8 us (2%)
    psum x1, waiting for transfers between devices, expert_block(): gate_up = lax.psum(gate_up, 'gy')  393 us
    all_gather x2, blocking collectives, merged(): gathered = jax.tree.map(lambda a: lax.all_gather(a, axis), part)  73.9 us
    while x24, local copies, waits for them, and re-layouts  48.4 us
    while x16, other arithmetic  35.7 us
    gather x8, local copies, waits for them, and re-layouts, visit_block(): queries[owning_block]  28.5 us
    all_gather x1, waiting for transfers between devices, merged(): gathered = jax.tree.map(lambda a: lax.all_gather(a, axis), part)  27.2 us
    gather x16, local copies, waits for them, and re-layouts, visit_block(): prob_block = jnp.exp(scores - new_max[owning_block]).astype(jnp.bfloat16)  19.4 us
    psum x1, blocking collectives, shards(): squares = lax.psum(jnp.sum(hidden_f * hidden_f, axis=1), 'gy')  19.3 us
  transfers between devices with their start and end apart: 5, of which 4 were waited for; matrix products, arithmetic and copies ran while one was open for 1% of the time, Pallas kernels for 0%

profile of v1, /device:TPU:0, one launch (start us, length us, event | category | flops | bytes accessed | tf_op | source)
XLA Modules:
  0.0 815.4 jit_solution(974354665612398548)
XLA Ops:
  6.5 7.0 reshape.212
  13.6 7.0 reshape_squeeze.10
  22.4 178.0 %while.35 = (s32[]{:T(128)}, f32[64,4,5]{2,1,0:T(4,128)S(1)}, f32[64,4,5]{2,1,0:T(4,128)S(1)}, f32[64,4,5,128]{3,0,2,1:T(8,128)}, s32[8,512]{1,0:T(8,128)}, /*in...) while((s32[]{:T(128)}, f32[64,4,5]{2,1,0:T(4,128)S(1)}, ...), condition=%wide.region_3.4_spmd.clone, body=%wide.region_0.3_spmd.clone.sunk | while | flops 176462592 | bytes 21555320 | solution.py:121
  23.1 3.6 gather_fusion
  26.7 4.5 copy.164
  44.4 3.6 gather_fusion
  48.0 4.5 copy.164
  66.8 3.6 gather_fusion
  70.4 4.5 copy.164
  92.8 4.5 copy.164
  115.2 4.5 copy.164
  137.6 4.5 copy.164
  160.0 4.5 copy.164
  182.4 4.5 copy.164
  202.2 38.6 %all-gather = f32[512,4,5]{2,1,0:T(4,128)S(1)} all-gather(f32[64,4,5]{2,1,0:T(4,128)S(1)} %get-tuple-element.232), channel_id=2, replica_groups=mesh['gx'=4,'gy'=8] {'gy'}, dimensions={0}, use_global_device_ids=true | all-gather | bytes 46080 | tf_op jit(solution)/shard_map/all_gather | solution.py:41
  240.9 35.2 %all-gather.1 = f32[512,4,5]{2,1,0:T(4,128)S(1)} all-gather(f32[64,4,5]{2,1,0:T(4,128)S(1)} %get-tuple-element.233), channel_id=3, replica_groups=mesh['gx'=4,'gy'=8] {'gy'}, dimensions={0}, use_global_device_ids=true | all-gather | bytes 46080 | tf_op jit(solution)/shard_map/all_gather | solution.py:41
  282.6 27.2 %all-gather.5.cloned.1.call-done = f32[512,4,5,128]{3,0,2,1:T(8,128)} async-done(((f32[64,4,5,128]{3,0,2,1:T(8,128)}), f32[512,4,5,128]{3,0,2,1:T(8,128)}) %all-gather.5.cloned.1.call-update) | async-done | bytes 5242896 | tf_op jit(solution)/shard_map/all_gather | solution.py:41
  311.4 20.6 %while.34 = (s32[]{:T(128)}, f32[64,4,5]{0,1,2:T(4,128)S(1)}, f32[64,4,5]{0,1,2:T(4,128)S(1)}, f32[64,4,5,128]{3,2,1,0:T(8,128)S(1)}, f32[8,64,4,5]{1,2,3,0:T(4,...) while((s32[]{:T(128)}, f32[64,4,5]{0,1,2:T(4,128)S(1)}, ...), condition=%wide.region_5.6_spmd, body=%wide.region_4.5_spmd.sunk | while | flops 499205 | bytes 3348631 | solution.py:46
  336.7 19.3 %psum.14 = f32[64]{0:T(128)S(1)} all-reduce(f32[64]{0:T(128)S(1)} %get-tuple-element.368), channel_id=1, replica_groups=mesh['gx'=4,'gy'=8] {'gy'}, use_global_device_ids=true, to_apply=%region_12.13 | all-reduce | flops 64 | bytes 512 | tf_op jit(solution)/shard_map/psum | solution.py:189
  358.7 12.1 %all_to_all.5 = bf16[4,16,12,320]{3,1,2,0:T(8,128)(2,1)S(1)} all-to-all(bf16[4,16,12,320]{3,1,2,0:T(8,128)(2,1)S(1)} %copy.105), channel_id=1, replica_groups=mesh['gx'=4,'gy'=8] {'gx'}, dimensions={0} | all-to-all | bytes 983040 | tf_op jit(solution)/shard_map/all_to_all | solution.py:211
  370.8 16.6 %fusion.23 = f32[4,16,12,3072]{3,2,0,1:T(8,128)} fusion(bf16[16,320,3072]{2,1,0:T(8,128)(2,1)} %param.26, bf16[4,16,12,320]{3,1,2,0:T(8,128)(2,1)S(1)} %all_to_all.5), kind=kOutput, calls=%fused_computation.44 | convolution fusion | flops 1509949440 | bytes 41385984 | tf_op jit(solution)/shard_map/sekd,edf->sekf/dot_general | solution.py:126
  388.3 392.8 %all-reduce.2.cloned.1.call-done = f32[4,16,12,3072]{3,2,0,1:T(8,128)} async-done(((f32[4,16,12,3072]{3,2,0,1:T(8,128)}), f32[4,16,12,3072]{3,2,0,1:T(8,128)}) %all-reduce.2.cloned.1.call-update) | async-done | bytes 9437200 | tf_op jit(solution)/shard_map/psum | solution.py:127
  781.2 11.6 %fusion.29 = bf16[16,4,12,320]{3,2,1,0:T(8,128)(2,1)S(1)} fusion(bf16[16,1536,320]{1,2,0:T(8,128)(2,1)} %param.27, f32[4,16,12,3072]{3,2,0,1:T(8,128)} %all-reduce.2.cloned.1.call-done), kind=kOutput, calls=%fused_computation.48 | convolution fusion | flops 762298368 | bytes 25657344 | tf_op jit(solution)/shard_map/sekf,efd->sekd/dot_general | solution.py:131
  796.9 4.8 collective-permute-done.1
  (310 shorter events, 181.5 us)
Async XLA Ops:
  6.5 329.4 %copy-start = (bf16[2560,320]{0,1:T(8,128)(2,1)S(1)}, bf16[2560,320]{0,1:T(8,128)(2,1)}, u32[]{:S(2)}) copy-start(bf16[2560,320]{0,1:T(8,128)(2,1)} %param.21) | copy-start | bytes 4915204
  6.5 303.3 %all-gather.5.cloned.1.call-start = ((), (), s32[]{:S(2)}) async-start(), calls=%async_computation.2 | async-start | bytes 5898240 | tf_op jit(solution)/shard_map/all_gather | solution.py:41
  13.6 7.5 copy-start.7
  13.6 8.8 %copy-start.1 = (bf16[64,2560]{1,0:T(8,128)(2,1)S(1)}, bf16[64,2560]{1,0:T(8,128)(2,1)}, u32[]{:S(2)}) copy-start(bf16[64,2560]{1,0:T(8,128)(2,1)} %param.16) | copy-start | bytes 983044
  22.4 179.4 %copy-start.8 = (s32[256,6]{0,1:T(8,128)S(1)}, s32[256,6]{0,1:T(8,128)}, u32[]{:S(2)}) copy-start(s32[256,6]{0,1:T(8,128)} %param.24) | copy-start | bytes 18436
  200.4 78.9 %copy-start.4 = (bf16[64,1024]{1,0:T(8,128)(2,1)S(1)}, bf16[64,1024]{1,0:T(8,128)(2,1)}, u32[]{:S(2)}) copy-start(bf16[64,1024]{1,0:T(8,128)(2,1)} %param.17) | copy-start | bytes 393220
  200.5 80.5 %copy-start.9 = (bf16[320]{0:T(512)(128)(2,1)S(1)}, bf16[320]{0:T(512)(128)(2,1)}, u32[]{:S(2)}) copy-start(bf16[320]{0:T(512)(128)(2,1)} %param.23) | copy-start | bytes 1924
  200.5 580.7 %all-reduce.2.cloned.1.call-start = ((), (), s32[]{:S(2)}) async-start(), calls=%async_computation.1 | async-start | bytes 25165824 | tf_op jit(solution)/shard_map/psum | solution.py:127
  276.2 1.0 copy-start.2
  311.4 24.6 %copy-start.5 = (bf16[64,320]{1,0:T(8,128)(2,1)S(1)}, bf16[64,320]{1,0:T(8,128)(2,1)}, u32[]{:S(2)}) copy-start(bf16[64,320]{1,0:T(8,128)(2,1)} %param.22) | copy-start | bytes 122884
  387.4 0.7 copy-start.6
  792.8 0.9 copy-start.3
  793.7 3.1 collective-permute-start
  793.9 7.7 collective-permute-start.1
  795.4 9.6 %collective-permute-start.2 = (bf16[1,16,12,320]{3,2,1,0:T(8,128)(2,1)S(1)}, bf16[1,16,12,320]{3,2,1,0:T(8,128)(2,1)S(1)}, u32[]{:S(2)}, u32[]{:S(2)}) collective-permute-start(bf16[1,16,12,320]{3,2,1,0:T(8,128)(2,1)S(1)} %get-tuple-element.363), channel_id=1, source_target_pairs={{0,24},{8,16},{16,8},{24,0},{1,25},{9,17},{17,9},{25,1},{2,26},{10... | collective-permute-start | bytes 368648 | tf_op jit(solution)/shard_map/ppermute | solution.py:30
Sparse Core Ops, SparseCore 0:
  200.6 109.1 all-gather.4
  387.6 393.5 all-reduce.1
